TPU v7x, 256 devices: a whole 4x4x8 slice. The times are simulated.
256 devices in a mesh: span: 8 (over z), ha: 8 (over x, core), wa: 4 (over y).
Axes of the slice: x: 4, y: 4, z: 8, core: 2. Of those that a mesh axis runs over, the one named last changes fastest.
Arguments:
- queries: bfloat16 [8, 3, 32, 48, 768], P('span', None, 'ha', 'wa'), may hold values from -5 to 5
- cache_keys: bfloat16 [8, 3, 32, 48, 768], P('span', None, 'ha', 'wa'), may hold values from -5 to 5
- cache_values: bfloat16 [8, 3, 32, 48, 768], P('span', None, 'ha', 'wa'), may hold values from -16 to 16
- grad_attended: bfloat16 [8, 3, 32, 48, 768], P('span', None, 'ha', 'wa'), may hold values from -16 to 16
- radius: int32 [6], replicated, may hold values from 1 to 2, as said below
- frame_count: int32 [8], replicated, may hold values from 1 to 3, as said below
Outputs:
- attended: bfloat16 [8, 3, 32, 48, 768], P('span', None, 'ha', 'wa')
- grad_queries: bfloat16 [8, 3, 32, 48, 768], P('span', None, 'ha', 'wa')
- grad_keys: bfloat16 [8, 3, 32, 48, 768], P('span', None, 'ha', 'wa')
- grad_values: bfloat16 [8, 3, 32, 48, 768], P('span', None, 'ha', 'wa')
Inputs may be any that keep to these rules, and one draw needn't show every extreme that they name: Some head has radius 2 and some other head has radius 1. Frame slots of block c at or past frame_count[c] hold padding; some block has all 3 slots live.
All inputs are finite; a program needn't handle non-finite values.
Results may differ from a plain program's by a relative error of at most 0.02.
Values may be sent and summed in bfloat16 or wider, within the bound.
A program may use at most 128 MiB of HBM per device.

v0:
```python
import math
import jax
import jax.numpy as jnp
from jax import lax
from jax.sharding import PartitionSpec as P

RMAX = 2


def padded(block, sides, width):
    for axis, dim in sides:
        count = lax.axis_size(axis)
        forward = [(i, i + 1) for i in range(count - 1)]
        backward = [(target, source) for source, target in forward]
        low = lax.ppermute(
            lax.slice_in_dim(block, block.shape[dim] - width, None, axis=dim), axis, forward
        )
        high = lax.ppermute(lax.slice_in_dim(block, 0, width, axis=dim), axis, backward)
        block = jnp.concatenate([low, block, high], axis=dim)
    return block


def near_table(radius, tile_h, tile_w, margin, first_row, first_col, full_h, full_w):
    rows_local = jnp.arange(tile_h)
    rows_wide = jnp.arange(tile_h + 2 * margin) - margin
    cols_local = jnp.arange(tile_w)
    cols_wide = jnp.arange(tile_w + 2 * margin) - margin
    gap_rows = jnp.abs(rows_local[:, None] - rows_wide[None, :])
    gap_cols = jnp.abs(cols_local[:, None] - cols_wide[None, :])
    inside_rows = (first_row + rows_wide >= 0) & (first_row + rows_wide < full_h)
    inside_cols = (first_col + cols_wide >= 0) & (first_col + cols_wide < full_w)
    reach = jnp.maximum(gap_rows[:, None, :, None], gap_cols[None, :, None, :])
    inside = inside_rows[:, None] & inside_cols[None, :]
    within = (reach[None] <= radius[:, None, None, None, None]) & inside[None, None, None]
    return within.reshape(
        radius.shape[0], tile_h * tile_w, (tile_h + 2 * margin) * (tile_w + 2 * margin)
    )


def with_frames(spatial, frame_live):
    heads, rows, columns = spatial.shape
    frames = frame_live.shape[0]
    joined = spatial[:, None, :, None, :] & frame_live[None, None, None, :, None]
    joined = jnp.broadcast_to(joined, (heads, frames, rows, frames, columns))
    return joined.reshape(heads, frames * rows, frames * columns)


def live_frames(frame_count, block_id, frames):
    picked = jnp.arange(frame_count.shape[0]) == block_id
    count = jnp.sum(jnp.where(picked, frame_count, 0))
    return jnp.arange(frames) < count


def over_tiles(advance, carried, piece):
    block_ids = jnp.arange(piece.shape[0], dtype=jnp.int32)

    def inner(current, item):
        return (advance(current, item[0], item[1]), None)

    result, _ = lax.scan(inner, carried, (piece, block_ids))
    return result


def shards(queries, cache_keys, cache_values, grad_attended, radius, frame_count):
    frames, tile_h, tile_w, width = queries.shape[1:]
    heads = radius.shape[0]
    depth = width // heads
    margin = RMAX
    scale = 1.0 / math.sqrt(depth)
    own_block = lax.axis_index("span")
    block_total = lax.axis_size("span")
    first_row = lax.axis_index("ha") * tile_h
    first_col = lax.axis_index("wa") * tile_w
    spatial = near_table(
        radius,
        tile_h,
        tile_w,
        margin,
        first_row,
        first_col,
        tile_h * lax.axis_size("ha"),
        tile_w * lax.axis_size("wa"),
    )
    local_rows = frames * tile_h * tile_w
    wide_rows = frames * (tile_h + 2 * margin) * (tile_w + 2 * margin)
    query_rows = queries.reshape(local_rows, heads, depth)
    key_local = cache_keys.reshape(local_rows, heads, depth)
    value_local = cache_values.reshape(local_rows, heads, depth)
    upstream = grad_attended.reshape(local_rows, heads, depth)
    key_mask = with_frames(
        jnp.transpose(spatial, (0, 2, 1)), live_frames(frame_count, own_block, frames)
    )
    bundle = jnp.concatenate([cache_keys, cache_values, queries, grad_attended], axis=4)

    def forward_step(carried, tile, block_id):

        def forward_run(current):
            top, total, accum = current
            key_rows = tile[..., :width].reshape(wide_rows, heads, depth)
            value_rows = tile[..., width : 2 * width].reshape(wide_rows, heads, depth)
            allowed = with_frames(spatial, live_frames(frame_count, block_id, frames))
            score = (
                jnp.einsum("qhd,khd->hqk", query_rows, key_rows, preferred_element_type=jnp.float32)
                * scale
            )
            score = jnp.where(allowed, score, -jnp.inf)
            new_top = jnp.maximum(top, jnp.max(score, axis=2))
            weight = jnp.exp(score - new_top[:, :, None])
            fading = jnp.exp(top - new_top)
            total = total * fading + jnp.sum(weight, axis=2)
            accum = accum * fading[:, :, None] + jnp.einsum(
                "hqk,khd->hqd",
                weight.astype(jnp.bfloat16),
                value_rows,
                preferred_element_type=jnp.float32,
            )
            return (new_top, total, accum)

        active = (block_id >= 0) & (block_id <= own_block)
        return lax.cond(active, forward_run, lambda current: current, carried)

    def query_grad_step(carried, tile, block_id):

        def query_run(current):
            key_rows = tile[..., :width].reshape(wide_rows, heads, depth)
            value_rows = tile[..., width : 2 * width].reshape(wide_rows, heads, depth)
            allowed = with_frames(spatial, live_frames(frame_count, block_id, frames))
            score = (
                jnp.einsum("qhd,khd->hqk", query_rows, key_rows, preferred_element_type=jnp.float32)
                * scale
            )
            prob = jnp.exp(jnp.where(allowed, score - log_total[:, :, None], -jnp.inf))
            push = jnp.einsum(
                "qhd,khd->hqk", upstream, value_rows, preferred_element_type=jnp.float32
            )
            slope = (prob * (push - delta[:, :, None])).astype(jnp.bfloat16)
            return current + jnp.einsum(
                "hqk,khd->hqd", slope, key_rows, preferred_element_type=jnp.float32
            )

        active = (block_id >= 0) & (block_id <= own_block)
        return lax.cond(active, query_run, lambda current: current, carried)

    def key_grad_step(carried, tile, block_id):

        def key_run(current):
            grad_k, grad_v = current
            asking = tile[..., -2 * width : -width].reshape(wide_rows, heads, depth)
            asking_grad = tile[..., -width:].reshape(wide_rows, heads, depth)
            stat_tile = lax.dynamic_index_in_dim(
                stats_all, jnp.clip(block_id, 0, block_total - 1), 0, keepdims=False
            )
            stat_rows = stat_tile.reshape(wide_rows, 2 * heads)
            row_lse = jnp.transpose(stat_rows[:, :heads])
            row_delta = jnp.transpose(stat_rows[:, heads:])
            score = (
                jnp.einsum("qhd,khd->hqk", asking, key_local, preferred_element_type=jnp.float32)
                * scale
            )
            prob = jnp.exp(jnp.where(key_mask, score - row_lse[:, :, None], -jnp.inf))
            grad_v = grad_v + jnp.einsum(
                "hqk,qhd->khd",
                prob.astype(jnp.bfloat16),
                asking_grad,
                preferred_element_type=jnp.float32,
            )
            push = jnp.einsum(
                "qhd,khd->hqk", asking_grad, value_local, preferred_element_type=jnp.float32
            )
            slope = (prob * (push - row_delta[:, :, None])).astype(jnp.bfloat16)
            grad_k = grad_k + jnp.einsum(
                "hqk,qhd->khd", slope, asking, preferred_element_type=jnp.float32
            )
            return (grad_k, grad_v)

        active = (block_id >= own_block) & (block_id < block_total)
        return lax.cond(active, key_run, lambda current: current, carried)

    start_state = (
        jnp.full((heads, local_rows), -jnp.inf, jnp.float32),
        jnp.zeros((heads, local_rows), jnp.float32),
        jnp.zeros((heads, local_rows, depth), jnp.float32),
    )
    everything = lax.all_gather(bundle, "span", axis=0, tiled=True)
    wide_all = padded(everything, (("ha", 2), ("wa", 3)), RMAX)
    top, total, accum = over_tiles(forward_step, start_state, wide_all)
    attended_rows = jnp.transpose((accum / total[:, :, None]).astype(jnp.bfloat16), (1, 0, 2))
    log_total = top + jnp.log(total)
    delta = jnp.einsum("qhd,qhd->hq", upstream, attended_rows, preferred_element_type=jnp.float32)
    stats = jnp.concatenate([jnp.transpose(log_total), jnp.transpose(delta)], axis=1)
    stats = stats.reshape(1, frames, tile_h, tile_w, 2 * heads)
    stat_wide = padded(stats, (("ha", 2), ("wa", 3)), RMAX)
    stats_all = lax.all_gather(stat_wide, "span", axis=0, tiled=True)
    query_start = jnp.zeros((heads, local_rows, depth), jnp.float32)
    key_start = (
        jnp.zeros((local_rows, heads, depth), jnp.float32),
        jnp.zeros((local_rows, heads, depth), jnp.float32),
    )
    grad_q = over_tiles(query_grad_step, query_start, wide_all)
    grad_k, grad_v = over_tiles(key_grad_step, key_start, wide_all)
    final = (1, frames, tile_h, tile_w, width)
    attended = attended_rows.reshape(final)
    grad_queries = jnp.transpose(grad_q * scale, (1, 0, 2)).astype(jnp.bfloat16).reshape(final)
    grad_keys = (grad_k * scale).astype(jnp.bfloat16).reshape(final)
    grad_values = grad_v.astype(jnp.bfloat16).reshape(final)
    return (attended, grad_queries, grad_keys, grad_values)


def solution(mesh):
    placed = (
        P("span", None, "ha", "wa", None),
        P("span", None, "ha", "wa", None),
        P("span", None, "ha", "wa", None),
        P("span", None, "ha", "wa", None),
        P(),
        P(),
    )
    return jax.shard_map(
        shards,
        mesh=mesh,
        in_specs=placed,
        out_specs=(
            P("span", None, "ha", "wa", None),
            P("span", None, "ha", "wa", None),
            P("span", None, "ha", "wa", None),
            P("span", None, "ha", "wa", None),
        ),
        check_vma=False,
    )
```

profile of v0, /device:TPU:2, one launch (start us, length us, event | category | flops | bytes accessed | tf_op | source)
XLA Modules:
  0.0 646.9 jit_solution(17913290227682815183)
XLA Ops:
  7.2 2.6 pad_maximum_fusion.4
  9.8 84.9 %all-gather.2.cloned.1.call-done = bf16[8,3,4,12,3072]{4,2,3,1,0:T(4,128)(2,1)} async-done(((bf16[1,3,4,12,3072]{4,2,3,1,0:T(4,128)(2,1)}), bf16[8,3,4,12,3072]{4,2,3,1,0:T(4,128)(2,1)}) %all-gather.2.cloned.1.call-update) | async-done | bytes 7077904 | tf_op jit(solution)/shard_map/all_gather | solution.py:184
  94.7 9.5 %fusion.57 = (bf16[8,3,2,12,3072]{4,2,3,1,0:T(2,128)(2,1)S(1)}, bf16[8,3,2,12,3072]{4,2,3,1,0:T(2,128)(2,1)S(1)}) fusion(bf16[8,3,4,12,3072]{4,2,3,1,0:T(4,128)(2,1)} %all-gather.2.cloned.1.call-done), kind=kLoop, calls=%fused_computation.100 | loop fusion | bytes 14155776 | tf_op jit(solution)/shard_map/slice | solution.py:16
  104.3 1.9 copy.85
  106.2 1.9 collective-permute-start
  108.2 3.8 copy.86
  112.0 4.4 collective-permute-start.1
  116.3 32.7 %collective-permute-done = bf16[8,3,2,12,3072]{4,0,3,2,1:T(8,128)(2,1)S(1)} collective-permute-done((bf16[8,3,2,12,3072]{4,0,3,2,1:T(8,128)(2,1)S(1)}, bf16[8,3,2,12,3072]{4,0,3,2,1:T(8,128)(2,1)S(1)}, u32[]{:S(2)}, u32[]{:S(2)}) %collective-permute-start) | collective-permute-done | bytes 3538976 | tf_op jit(solution)/shard_map/ppermute | solution.py:15
  149.0 3.6 copy.87
  152.7 2.5 collective-permute-done.1
  155.2 5.6 copy.88
  160.9 5.3 pad_maximum_fusion.3
  166.2 4.8 collective-permute-start.2
  175.4 2.0 reshape.221
  179.1 2.0 reshape.223
  184.8 1.9 reshape.225
  188.4 1.9 reshape.228
  198.0 22.7 %collective-permute-done.2 = bf16[8,3,8,2,3072]{4,2,3,1,0:T(8,128)(2,1)} collective-permute-done((bf16[8,3,8,2,3072]{4,2,3,1,0:T(8,128)(2,1)}, bf16[8,3,8,2,3072]{4,2,3,1,0:T(8,128)(2,1)}, u32[]{:S(2)}, u32[]{:S(2)}) %collective-permute-start.2) | collective-permute-done | bytes 2359328 | tf_op jit(solution)/shard_map/ppermute | solution.py:15
  220.7 6.0 collective-permute-done.3
  226.8 13.9 %pad_maximum_fusion = bf16[8,3,8,16,3072]{4,2,3,1,0:T(8,128)(2,1)S(1)} fusion(bf16[8,3,8,2,3072]{4,2,3,1,0:T(8,128)(2,1)} %collective-permute-done.3, bf16[8,3,2,12,3072]{4,2,3,1,0:T(2,128)(2,1)} %copy-done, bf16[8,3,4,12,3072]{4,2,3,1,0:T(4,128)(2,1)} %all-gather.2.cloned.1.call-done, bf16[8,3,2,12,3072]{4,2,3,1,0:T(2,128)(2,1)S(1)} %copy.87, ...), kind=kLoop, calls=%fused_computation.67 | loop fusion | flops 94371840 | bytes 37748736 | tf_op jit(solution)/shard_map/concatenate | solution.py:19
  240.7 12.6 %copy.90 = bf16[8,3,8,16,3072]{4,3,2,1,0:T(8,128)(2,1)} copy(bf16[8,3,8,16,3072]{4,2,3,1,0:T(8,128)(2,1)S(1)} %pad_maximum_fusion) | data formatting | bytes 37748736
  253.4 26.6 %while.42 = (s32[]{:T(128)}, f32[6,144]{1,0:T(8,128)S(1)}, f32[6,144]{1,0:T(8,128)S(1)}, f32[6,144,128]{2,1,0:T(8,128)S(1)}, s32[8]{0:T(128)S(1)}, /*index=5*/s3...) while((s32[]{:T(128)}, f32[6,144]{1,0:T(8,128)S(1)}, ...), condition=%wide.region_6.7_spmd.clone, body=%wide.region_0.6_spmd.clone.sunk | while | flops 172599008 | bytes 17480200 | solution.py:60
  255.3 11.1 %conditional.9 = ((f32[6,144]{1,0:T(8,128)S(1)}, f32[6,144]{1,0:T(8,128)S(1)}, f32[6,144,128]{2,1,0:T(8,128)S(1)})) conditional(s32[]{:T(128)} %convert_element_type.76, (f32[6,144]{1,0:T(8,128)S(1)}, f32[6,144]{1,0:T(8,128)S(1)}, f32[6,144,128]{2,1,0:T(8,128)S(1)}) %tuple.115, (s32[4,12,8,16]{3,2,1,0:T(8,128)S(1)}, s32[]{:T(128)}, s32[8]{0:T(128)}, ...), branch_computations={%region_1.1_spmd, %region_2.0_spmd} | conditional | flops 172599008 | bytes 17479918 | solution.py:120
  282.9 2.2 collective-permute-start.4
  285.1 3.5 collective-permute-start.5
  290.0 29.6 %while.43 = (s32[]{:T(128)}, f32[6,144,128]{2,1,0:T(8,128)}, s32[8]{0:T(128)}, s32[]{:T(128)}, s32[8]{0:T(128)}, /*index=5*/bf16[8,3,8,16,3072]{4,3,2,1,0:T(8,12...) while((s32[]{:T(128)}, f32[6,144,128]{2,1,0:T(8,128)}, ...), condition=%wide.region_11.12_spmd.clone, body=%wide.region_7.11_spmd.clone.sunk | while | flops 257089568 | bytes 18095392 | solution.py:60
  292.3 11.0 %conditional.10 = (f32[6,144,128]{2,1,0:T(8,128)}) conditional(s32[]{:T(128)} %convert_element_type.77, f32[6,144,128]{2,1,0:T(8,128)} %get-tuple-element.945, (s32[4,12,8,16]{3,2,1,0:T(8,128)S(1)}, s32[]{:T(128)}, s32[8]{0:T(128)}, bf16[8,3,8,16,3072]{4,3,2,1,0:T(8,128)(2,1)}, s32[]{:T(128)}, /*index=5*/bf16[144,6,128]{2,0,1:T(8,128)(2,1)}, ...), branch_computations={%region_8.8_spmd, %region_9.10_spmd} | conditional | flops 257089568 | bytes 18095118 | solution.py:142
  300.6 2.7 fusion.23
  320.7 2.0 collective-permute-start.6
  327.4 2.8 collective-permute-done.7
  331.2 180.3 %all_gather.7 = f32[8,3,8,16,12]{3,2,4,1,0:T(8,128)S(1)} all-gather(f32[1,3,8,16,12]{3,2,4,1,0:T(8,128)S(1)} %copy.99), channel_id=1, replica_groups=mesh['span'=8,'ha'=8,'wa'=4] {'span'}, dimensions={0}, use_global_device_ids=true | all-gather | bytes 165888 | tf_op jit(solution)/shard_map/all_gather | solution.py:193
  513.5 122.9 %while.44 = (s32[]{:T(128)}, f32[144,6,128]{2,0,1:T(8,128)S(1)}, f32[144,6,128]{2,0,1:T(8,128)}, s32[8]{0:T(128)S(1)}, s32[]{:T(128)}, /*index=5*/bf16[8,3,8,16,...) while((s32[]{:T(128)}, f32[144,6,128]{2,0,1:T(8,128)S(1)}, ...), condition=%wide.region_16.17_spmd.clone, body=%wide.region_13.16_spmd.clone.sunk | while | flops 342282240 | bytes 23095652 | solution.py:60
  515.4 13.5 %conditional.11 = ((f32[144,6,128]{2,0,1:T(8,128)S(1)}, f32[144,6,128]{2,0,1:T(8,128)})) conditional(s32[]{:T(128)} %convert_element_type.78, (f32[144,6,128]{2,0,1:T(8,128)S(1)}, f32[144,6,128]{2,0,1:T(8,128)}) %tuple.120, (bf16[8,3,8,16,3072]{4,3,2,1,0:T(8,128)(2,1)}, s32[]{:T(128)}, bf16[144,6,128]{2,0,1:T(8,128)(2,1)}, s32[]{:T(128)}, ...), branch_computations={%region_14.14_spmd, %region_15.15_spmd} | conditional | flops 342282240 | bytes 23095408 | solution.py:177
  515.4 2.0 dynamic-slice_bitcast_fusion.2
  524.1 2.6 fusion.40
  526.6 2.2 fusion.41
  530.8 13.5 %conditional.11 = ((f32[144,6,128]{2,0,1:T(8,128)S(1)}, f32[144,6,128]{2,0,1:T(8,128)})) conditional(s32[]{:T(128)} %convert_element_type.78, (f32[144,6,128]{2,0,1:T(8,128)S(1)}, f32[144,6,128]{2,0,1:T(8,128)}) %tuple.120, (bf16[8,3,8,16,3072]{4,3,2,1,0:T(8,128)(2,1)}, s32[]{:T(128)}, bf16[144,6,128]{2,0,1:T(8,128)(2,1)}, s32[]{:T(128)}, ...), branch_computations={%region_14.14_spmd, %region_15.15_spmd} | conditional | flops 342282240 | bytes 23095408 | solution.py:177
  530.8 2.0 dynamic-slice_bitcast_fusion.2
  539.4 2.6 fusion.40
  542.0 2.2 fusion.41
  546.1 13.5 %conditional.11 = ((f32[144,6,128]{2,0,1:T(8,128)S(1)}, f32[144,6,128]{2,0,1:T(8,128)})) conditional(s32[]{:T(128)} %convert_element_type.78, (f32[144,6,128]{2,0,1:T(8,128)S(1)}, f32[144,6,128]{2,0,1:T(8,128)}) %tuple.120, (bf16[8,3,8,16,3072]{4,3,2,1,0:T(8,128)(2,1)}, s32[]{:T(128)}, bf16[144,6,128]{2,0,1:T(8,128)(2,1)}, s32[]{:T(128)}, ...), branch_computations={%region_14.14_spmd, %region_15.15_spmd} | conditional | flops 342282240 | bytes 23095408 | solution.py:177
  546.1 2.0 dynamic-slice_bitcast_fusion.2
  554.8 2.6 fusion.40
  557.4 2.2 fusion.41
  561.5 13.5 %conditional.11 = ((f32[144,6,128]{2,0,1:T(8,128)S(1)}, f32[144,6,128]{2,0,1:T(8,128)})) conditional(s32[]{:T(128)} %convert_element_type.78, (f32[144,6,128]{2,0,1:T(8,128)S(1)}, f32[144,6,128]{2,0,1:T(8,128)}) %tuple.120, (bf16[8,3,8,16,3072]{4,3,2,1,0:T(8,128)(2,1)}, s32[]{:T(128)}, bf16[144,6,128]{2,0,1:T(8,128)(2,1)}, s32[]{:T(128)}, ...), branch_computations={%region_14.14_spmd, %region_15.15_spmd} | conditional | flops 342282240 | bytes 23095408 | solution.py:177
  561.5 2.0 dynamic-slice_bitcast_fusion.2
  570.2 2.6 fusion.40
  572.7 2.2 fusion.41
  576.9 13.5 %conditional.11 = ((f32[144,6,128]{2,0,1:T(8,128)S(1)}, f32[144,6,128]{2,0,1:T(8,128)})) conditional(s32[]{:T(128)} %convert_element_type.78, (f32[144,6,128]{2,0,1:T(8,128)S(1)}, f32[144,6,128]{2,0,1:T(8,128)}) %tuple.120, (bf16[8,3,8,16,3072]{4,3,2,1,0:T(8,128)(2,1)}, s32[]{:T(128)}, bf16[144,6,128]{2,0,1:T(8,128)(2,1)}, s32[]{:T(128)}, ...), branch_computations={%region_14.14_spmd, %region_15.15_spmd} | conditional | flops 342282240 | bytes 23095408 | solution.py:177
  576.9 2.0 dynamic-slice_bitcast_fusion.2
  585.5 2.6 fusion.40
  588.1 2.2 fusion.41
  592.2 13.5 %conditional.11 = ((f32[144,6,128]{2,0,1:T(8,128)S(1)}, f32[144,6,128]{2,0,1:T(8,128)})) conditional(s32[]{:T(128)} %convert_element_type.78, (f32[144,6,128]{2,0,1:T(8,128)S(1)}, f32[144,6,128]{2,0,1:T(8,128)}) %tuple.120, (bf16[8,3,8,16,3072]{4,3,2,1,0:T(8,128)(2,1)}, s32[]{:T(128)}, bf16[144,6,128]{2,0,1:T(8,128)(2,1)}, s32[]{:T(128)}, ...), branch_computations={%region_14.14_spmd, %region_15.15_spmd} | conditional | flops 342282240 | bytes 23095408 | solution.py:177
  592.2 2.0 dynamic-slice_bitcast_fusion.2
  600.9 2.6 fusion.40
  603.5 2.2 fusion.41
  607.6 13.5 %conditional.11 = ((f32[144,6,128]{2,0,1:T(8,128)S(1)}, f32[144,6,128]{2,0,1:T(8,128)})) conditional(s32[]{:T(128)} %convert_element_type.78, (f32[144,6,128]{2,0,1:T(8,128)S(1)}, f32[144,6,128]{2,0,1:T(8,128)}) %tuple.120, (bf16[8,3,8,16,3072]{4,3,2,1,0:T(8,128)(2,1)}, s32[]{:T(128)}, bf16[144,6,128]{2,0,1:T(8,128)(2,1)}, s32[]{:T(128)}, ...), branch_computations={%region_14.14_spmd, %region_15.15_spmd} | conditional | flops 342282240 | bytes 23095408 | solution.py:177
  607.6 2.0 dynamic-slice_bitcast_fusion.2
  616.3 2.6 fusion.40
  618.8 2.2 fusion.41
  622.9 13.5 %conditional.11 = ((f32[144,6,128]{2,0,1:T(8,128)S(1)}, f32[144,6,128]{2,0,1:T(8,128)})) conditional(s32[]{:T(128)} %convert_element_type.78, (f32[144,6,128]{2,0,1:T(8,128)S(1)}, f32[144,6,128]{2,0,1:T(8,128)}) %tuple.120, (bf16[8,3,8,16,3072]{4,3,2,1,0:T(8,128)(2,1)}, s32[]{:T(128)}, bf16[144,6,128]{2,0,1:T(8,128)(2,1)}, s32[]{:T(128)}, ...), branch_computations={%region_14.14_spmd, %region_15.15_spmd} | conditional | flops 342282240 | bytes 23095408 | solution.py:177
  623.0 2.0 dynamic-slice_bitcast_fusion.2
  631.6 2.6 fusion.40
  634.2 2.2 fusion.41
  (267 shorter events, 121.1 us)
Async XLA Ops:
  7.2 87.6 %all-gather.2.cloned.1.call-start = ((), (), s32[]{:S(2)}) async-start(), calls=%async_computation | async-start | bytes 7962624 | tf_op jit(solution)/shard_map/all_gather | solution.py:184
  106.2 42.8 %collective-permute-start = (bf16[8,3,2,12,3072]{4,0,3,2,1:T(8,128)(2,1)S(1)}, bf16[8,3,2,12,3072]{4,0,3,2,1:T(8,128)(2,1)S(1)}, u32[]{:S(2)}, u32[]{:S(2)}) collective-permute-start(bf16[8,3,2,12,3072]{4,0,3,2,1:T(8,128)(2,1)S(1)} %copy.85), channel_id=1, source_target_pairs={{0,4},{4,8},{8,12},{12,16},{16,20},{20,24},{24,28},{1,5},{5,9},{9,... | collective-permute-start | bytes 10616840 | tf_op jit(solution)/shard_map/ppermute | solution.py:15
  108.1 52.7 %slice-start = ((s8[7077888]{0:T(1024)(128)(4,1)}), s8[4194304]{0:T(1024)(128)(4,1)S(1)}, s32[]{:S(2)}) async-start(s8[7077888]{0:T(1024)(128)(4,1)} %bitcast.91), calls=%async_computation.1 | async-start | bytes 8388608
  112.0 48.9 %slice-start.1 = ((s8[7077888]{0:T(1024)(128)(4,1)}), s8[2883584]{0:T(1024)(128)(4,1)S(1)}, s32[]{:S(2)}) async-start(s8[7077888]{0:T(1024)(128)(4,1)} %bitcast.91), calls=%async_computation.2 | async-start | bytes 5767168
  112.0 43.2 %collective-permute-start.1 = (bf16[8,3,2,12,3072]{4,0,3,2,1:T(8,128)(2,1)}, bf16[8,3,2,12,3072]{4,0,3,2,1:T(8,128)(2,1)}, u32[]{:S(2)}, u32[]{:S(2)}) collective-permute-start(bf16[8,3,2,12,3072]{4,0,3,2,1:T(8,128)(2,1)} %copy.86), channel_id=1, source_target_pairs={{4,0},{8,4},{12,8},{16,12},{20,16},{24,20},{28,24},{5,1},{9,5},{13... | collective-permute-start | bytes 10616840 | tf_op jit(solution)/shard_map/ppermute | solution.py:18
  160.8 5.3 copy-start
  160.8 11.6 %copy-start.5 = (bf16[1,3,4,12,768]{4,2,3,1,0:T(4,128)(2,1)S(1)}, bf16[1,3,4,12,768]{4,2,3,1,0:T(4,128)(2,1)}, u32[]{:S(2)}) copy-start(bf16[1,3,4,12,768]{4,2,3,1,0:T(4,128)(2,1)} %param.18) | copy-start | bytes 663556
  160.9 12.3 %copy-start.6 = (bf16[1,3,4,12,768]{4,2,3,1,0:T(4,128)(2,1)S(1)}, bf16[1,3,4,12,768]{4,2,3,1,0:T(4,128)(2,1)}, u32[]{:S(2)}) copy-start(bf16[1,3,4,12,768]{4,2,3,1,0:T(4,128)(2,1)} %param.21) | copy-start | bytes 663556
  160.9 13.0 %copy-start.7 = (bf16[1,3,4,12,768]{4,2,3,1,0:T(4,128)(2,1)S(1)}, bf16[1,3,4,12,768]{4,2,3,1,0:T(4,128)(2,1)}, u32[]{:S(2)}) copy-start(bf16[1,3,4,12,768]{4,2,3,1,0:T(4,128)(2,1)} %param.19) | copy-start | bytes 663556
  160.9 13.8 %copy-start.8 = (bf16[1,3,4,12,768]{4,2,3,1,0:T(4,128)(2,1)S(1)}, bf16[1,3,4,12,768]{4,2,3,1,0:T(4,128)(2,1)}, u32[]{:S(2)}) copy-start(bf16[1,3,4,12,768]{4,2,3,1,0:T(4,128)(2,1)} %param.20) | copy-start | bytes 663556
  166.2 54.5 %collective-permute-start.2 = (bf16[8,3,8,2,3072]{4,2,3,1,0:T(8,128)(2,1)}, bf16[8,3,8,2,3072]{4,2,3,1,0:T(8,128)(2,1)}, u32[]{:S(2)}, u32[]{:S(2)}) collective-permute-start(bf16[8,3,8,2,3072]{4,2,3,1,0:T(8,128)(2,1)} %get-tuple-element.644), channel_id=1, source_target_pairs={{0,1},{1,2},{2,3},{4,5},{5,6},{6,7},{8,9},{9,10},{10,11},{12,13},{... | collective-permute-start | bytes 7077896 | tf_op jit(solution)/shard_map/ppermute | solution.py:15
  170.9 55.8 %collective-permute-start.3 = (bf16[8,3,8,2,3072]{4,2,3,1,0:T(8,128)(2,1)}, bf16[8,3,8,2,3072]{4,2,3,1,0:T(8,128)(2,1)}, u32[]{:S(2)}, u32[]{:S(2)}) collective-permute-start(bf16[8,3,8,2,3072]{4,2,3,1,0:T(8,128)(2,1)} %get-tuple-element.645), channel_id=1, source_target_pairs={{1,0},{2,1},{3,2},{5,4},{6,5},{7,6},{9,8},{10,9},{11,10},{13,12},{... | collective-permute-start | bytes 7077896 | tf_op jit(solution)/shard_map/ppermute | solution.py:18
  175.4 21.0 %copy-start.11 = (s32[6]{0:T(128)S(1)}, s32[6]{0:T(128)}, u32[]{:S(2)}) copy-start(s32[6]{0:T(128)} %param.22) | copy-start | bytes 76
  183.2 10.6 %copy-start.12 = (pred[128]{0:T(512)(128)(4,1)S(1)}, pred[128]{0:T(512)(128)(4,1)}, u32[]{:S(2)}) copy-start(pred[128]{0:T(512)(128)(4,1)} %and.135) | copy-start | bytes 388
  240.7 12.7 %copy-start.1 = (s32[4,12,8,16]{3,2,1,0:T(8,128)S(1)}, s32[4,12,8,16]{3,2,1,0:T(8,128)}, u32[]{:S(2)}) copy-start(s32[4,12,8,16]{3,2,1,0:T(8,128)} %broadcast_maximum_fusion) | copy-start | bytes 73732
  282.9 36.7 %collective-permute-start.4 = (f32[1,3,2,12,12]{3,2,1,4,0:T(2,128)}, f32[1,3,2,12,12]{3,2,1,4,0:T(2,128)}, u32[]{:S(2)}, u32[]{:S(2)}) collective-permute-start(f32[1,3,2,12,12]{3,2,1,4,0:T(2,128)} %get-tuple-element.652), channel_id=1, source_target_pairs={{0,4},{4,8},{8,12},{12,16},{16,20},{20,24},{24,28},{1,5},{5,9},{9,... | collective-permute-start | bytes 10376 | tf_op jit(solution)/shard_map/ppermute | solution.py:15
  285.1 34.5 %collective-permute-start.5 = (f32[1,3,2,12,12]{3,2,1,4,0:T(2,128)}, f32[1,3,2,12,12]{3,2,1,4,0:T(2,128)}, u32[]{:S(2)}, u32[]{:S(2)}) collective-permute-start(f32[1,3,2,12,12]{3,2,1,4,0:T(2,128)} %get-tuple-element.653), channel_id=1, source_target_pairs={{4,0},{8,4},{12,8},{16,12},{20,16},{24,20},{28,24},{5,1},{9,5},{13... | collective-permute-start | bytes 10376 | tf_op jit(solution)/shard_map/ppermute | solution.py:18
  294.1 0.9 copy-start.4
  295.5 5.1 copy-start.10
  319.6 6.6 %copy-start.9 = (bf16[144,6,128]{2,0,1:T(8,128)(2,1)S(1)}, bf16[144,6,128]{2,0,1:T(8,128)(2,1)}, u32[]{:S(2)}) copy-start(bf16[144,6,128]{2,0,1:T(8,128)(2,1)} %get-tuple-element.649) | copy-start | bytes 663556
  320.7 6.7 %collective-permute-start.6 = (f32[1,3,8,2,12]{3,2,1,4,0:T(8,128)S(1)}, f32[1,3,8,2,12]{3,2,1,4,0:T(8,128)S(1)}, u32[]{:S(2)}, u32[]{:S(2)}) collective-permute-start(f32[1,3,8,2,12]{3,2,1,4,0:T(8,128)S(1)} %get-tuple-element.650), channel_id=1, source_target_pairs={{0,1},{1,2},{2,3},{4,5},{5,6},{6,7},{8,9},{9,10},{10,11},{12,13},{... | collective-permute-start | bytes 6920 | tf_op jit(solution)/shard_map/ppermute | solution.py:15
  322.7 7.5 %collective-permute-start.7 = (f32[1,3,8,2,12]{3,2,1,4,0:T(8,128)S(1)}, f32[1,3,8,2,12]{3,2,1,4,0:T(8,128)S(1)}, u32[]{:S(2)}, u32[]{:S(2)}) collective-permute-start(f32[1,3,8,2,12]{3,2,1,4,0:T(8,128)S(1)} %get-tuple-element.651), channel_id=1, source_target_pairs={{1,0},{2,1},{3,2},{5,4},{6,5},{7,6},{9,8},{10,9},{11,10},{13,12},{... | collective-permute-start | bytes 6920 | tf_op jit(solution)/shard_map/ppermute | solution.py:18
  515.4 2.0 copy-start.2
  526.6 2.2 copy-start.3
  530.8 2.0 copy-start.2
  542.0 2.2 copy-start.3
  546.1 2.0 copy-start.2
  557.4 2.2 copy-start.3
  561.5 2.0 copy-start.2
  572.7 2.2 copy-start.3
  576.9 2.0 copy-start.2
  588.1 2.2 copy-start.3
  592.2 2.0 copy-start.2
  603.5 2.2 copy-start.3
  607.6 2.0 copy-start.2
  618.8 2.2 copy-start.3
  623.0 2.0 copy-start.2
  634.2 2.2 copy-start.3
Sparse Core Ops, SparseCore 0:
  10.0 84.7 all-gather.1
where the time goes:
time: 655 us; the launch traced here: 647 us
  blocking collectives  180 us (27%)
  waiting for transfers between devices  152 us (23%)
  local copies, waits for them, and re-layouts  147 us (22%)
  matrix products  55.1 us (8%)
  other arithmetic  39.6 us (6%)
  loops' own time  36.7 us (6%)
  starting transfers between devices  21.6 us (3%)
  between operations  14.7 us (2%)
    all_gather x1, blocking collectives, shards(): stats_all = lax.all_gather(stat_wide, 'span', axis=0, tiled=True)  180 us
    all_gather x1, waiting for transfers between devices, shards(): everything = lax.all_gather(bundle, 'span', axis=0, tiled=True)  84.9 us
    ppermute x4, waiting for transfers between devices, padded(): lax.ppermute(lax.slice_in_dim(block, block.shape[dim] - width, None, axis...  55.4 us
    another operation x3, loops' own time, over_tiles(): result, _ = lax.scan(inner, carried, (piece, block_ids))  30.3 us
    unnamed x36, local copies, waits for them, and re-layouts  26.6 us
    dot_general x8, matrix products, key_run(): jnp.einsum('hqk,qhd->khd', slope, asking, preferred_element_type=jnp.floa...  20.5 us
    squeeze x10, local copies, waits for them, and re-layouts, over_tiles(): result, _ = lax.scan(inner, carried, (piece, block_ids))  19.7 us
    dynamic_slice x24, local copies, waits for them, and re-layouts, over_tiles(): result, _ = lax.scan(inner, carried, (piece, block_ids))  18.6 us
  transfers between devices with their start and end apart: 9, of which 6 were waited for; matrix products, arithmetic and copies ran while one was open for 9% of the time, Pallas kernels for 0%

commit v1 on v0

--- a/solution.py
+++ b/solution.py
@@ -181,7 +181,9 @@
         jnp.zeros((heads, local_rows), jnp.float32),
         jnp.zeros((heads, local_rows, depth), jnp.float32),
     )
-    everything = lax.all_gather(bundle, "span", axis=0, tiled=True)
+    everything = jnp.concatenate(
+        lax.all_to_all(jnp.stack([bundle] * lax.axis_size("span")), "span", 0, 0), axis=0
+    )
     wide_all = padded(everything, (("ha", 2), ("wa", 3)), RMAX)
     top, total, accum = over_tiles(forward_step, start_state, wide_all)
     attended_rows = jnp.transpose((accum / total[:, :, None]).astype(jnp.bfloat16), (1, 0, 2))

time: 655 us -> 723 us (1.10)
  blocking collectives: 180 us -> 344 us
  waiting for transfers between devices: 152 us -> 66.8 us
  between operations: 14.7 us -> 1.24 us
    all_to_all x0 -> x1, blocking collectives: none -> 166 us  [shards(): lax.all_to_all(jnp.stack([bundle] * lax.axis_size('span')), 'span', 0, 0)]
    all_gather x1 -> x0, waiting for transfers between devices: 84.9 us -> none  [shards(): everything = lax.all_gather(bundle, 'span', axis=0, tiled=True)]
    unnamed x36 -> x34, local copies, waits for them, and re-layouts: 26.6 us -> 26.6 us
  transfers between devices with their start and end apart: 9 -> 8, of which waited for: 6 -> 5; matrix products, arithmetic and copies ran while one was open for 9% -> 8% of each run, Pallas kernels for 0% -> 0%
where the time goes in v1:
time: 723 us; the launch traced here: 714 us
  blocking collectives  344 us (48%)
  local copies, waits for them, and re-layouts  148 us (20%)
  waiting for transfers between devices  66.8 us (9%)
  matrix products  55.2 us (8%)
  other arithmetic  39.6 us (5%)
  loops' own time  37.5 us (5%)
  starting transfers between devices  21.5 us (3%)
    all_gather x1, blocking collectives, shards(): stats_all = lax.all_gather(stat_wide, 'span', axis=0, tiled=True)  177 us
    all_to_all x1, blocking collectives, shards(): lax.all_to_all(jnp.stack([bundle] * lax.axis_size('span')), 'span', 0, 0)  166 us
    ppermute x4, waiting for transfers between devices, padded(): lax.ppermute(lax.slice_in_dim(block, block.shape[dim] - width, None, axis...  55.6 us
    another operation x3, loops' own time, over_tiles(): result, _ = lax.scan(inner, carried, (piece, block_ids))  31.1 us
    unnamed x34, local copies, waits for them, and re-layouts  26.6 us
    dot_general x8, matrix products, key_run(): jnp.einsum('hqk,qhd->khd', slope, asking, preferred_element_type=jnp.floa...  20.7 us
    squeeze x10, local copies, waits for them, and re-layouts, over_tiles(): result, _ = lax.scan(inner, carried, (piece, block_ids))  19.7 us
    dynamic_slice x24, local copies, waits for them, and re-layouts, over_tiles(): result, _ = lax.scan(inner, carried, (piece, block_ids))  19.4 us
  transfers between devices with their start and end apart: 8, of which 5 were waited for; matrix products, arithmetic and copies ran while one was open for 8% of the time, Pallas kernels for 0%

profile of v1, /device:TPU:2, one launch (start us, length us, event | category | flops | bytes accessed | tf_op | source)
XLA Modules:
  0.0 713.6 jit_solution(4891781726859204003)
XLA Ops:
  0.6 2.6 maximum_bitcast_fusion
  3.2 4.3 stack.2
  7.6 166.2 %all_to_all.5 = bf16[8,1,3,4,12,3072]{5,3,4,2,1,0:T(4,128)(2,1)S(1)} all-to-all(bf16[8,1,3,4,12,3072]{5,3,4,2,1,0:T(4,128)(2,1)S(1)} %stack.2), channel_id=1, replica_groups=mesh['span'=8,'ha'=8,'wa'=4] {'span'}, dimensions={0} | all-to-all | bytes 14155776 | tf_op jit(solution)/shard_map/all_to_all | solution.py:185
  173.8 5.0 fusion.57
  178.8 1.9 copy.79
  182.6 3.8 copy.80
  186.4 4.1 collective-permute-start.1
  190.6 33.0 %collective-permute-done = bf16[8,3,2,12,3072]{4,0,3,2,1:T(8,128)(2,1)S(1)} collective-permute-done((bf16[8,3,2,12,3072]{4,0,3,2,1:T(8,128)(2,1)S(1)}, bf16[8,3,2,12,3072]{4,0,3,2,1:T(8,128)(2,1)S(1)}, u32[]{:S(2)}, u32[]{:S(2)}) %collective-permute-start) | collective-permute-done | bytes 3538976 | tf_op jit(solution)/shard_map/ppermute | solution.py:15
  223.5 3.6 copy.81
  227.2 2.2 collective-permute-done.1
  229.4 5.6 copy.82
  235.1 5.3 pad_maximum_fusion.3
  240.4 4.9 collective-permute-start.2
  249.7 2.0 reshape.228
  259.1 2.0 reshape.232
  262.7 1.9 reshape.235
  272.3 22.7 %collective-permute-done.2 = bf16[8,3,8,2,3072]{4,2,3,1,0:T(8,128)(2,1)} collective-permute-done((bf16[8,3,8,2,3072]{4,2,3,1,0:T(8,128)(2,1)}, bf16[8,3,8,2,3072]{4,2,3,1,0:T(8,128)(2,1)}, u32[]{:S(2)}, u32[]{:S(2)}) %collective-permute-start.2) | collective-permute-done | bytes 2359328 | tf_op jit(solution)/shard_map/ppermute | solution.py:15
  295.0 6.1 collective-permute-done.3
  301.1 13.9 %pad_maximum_fusion = bf16[8,3,8,16,3072]{4,2,3,1,0:T(8,128)(2,1)S(1)} fusion(bf16[8,3,8,2,3072]{4,2,3,1,0:T(8,128)(2,1)} %collective-permute-done.3, bf16[8,3,2,12,3072]{4,2,3,1,0:T(2,128)(2,1)} %copy-done.1, bf16[8,3,4,12,3072]{4,2,3,1,0:T(4,128)(2,1)} %bitcast.96, bf16[8,3,2,12,3072]{4,2,3,1,0:T(2,128)(2,1)S(1)} %copy.81, ...), kind=kLoop, calls=%fused_computation.67 | loop fusion | flops 94371840 | bytes 37748736 | tf_op jit(solution)/shard_map/concatenate | solution.py:19
  315.0 12.6 %copy.84 = bf16[8,3,8,16,3072]{4,3,2,1,0:T(8,128)(2,1)} copy(bf16[8,3,8,16,3072]{4,2,3,1,0:T(8,128)(2,1)S(1)} %pad_maximum_fusion) | data formatting | bytes 37748736
  327.7 26.6 %while.42 = (s32[]{:T(128)}, f32[6,144]{1,0:T(8,128)S(1)}, f32[6,144]{1,0:T(8,128)S(1)}, f32[6,144,128]{2,1,0:T(8,128)S(1)}, s32[8]{0:T(128)S(1)}, /*index=5*/s3...) while((s32[]{:T(128)}, f32[6,144]{1,0:T(8,128)S(1)}, ...), condition=%wide.region_6.7_spmd.clone, body=%wide.region_0.6_spmd.clone.sunk | while | flops 172599008 | bytes 17480200 | solution.py:60
  329.6 11.2 %conditional.9 = ((f32[6,144]{1,0:T(8,128)S(1)}, f32[6,144]{1,0:T(8,128)S(1)}, f32[6,144,128]{2,1,0:T(8,128)S(1)})) conditional(s32[]{:T(128)} %convert_element_type.76, (f32[6,144]{1,0:T(8,128)S(1)}, f32[6,144]{1,0:T(8,128)S(1)}, f32[6,144,128]{2,1,0:T(8,128)S(1)}) %tuple.115, (s32[4,12,8,16]{3,2,1,0:T(8,128)S(1)}, s32[]{:T(128)}, s32[8]{0:T(128)}, ...), branch_computations={%region_1.1_spmd, %region_2.0_spmd} | conditional | flops 172599008 | bytes 17479918 | solution.py:120
  332.9 1.9 fusion.14
  357.3 2.2 collective-permute-start.4
  359.5 3.5 collective-permute-start.5
  364.4 31.3 %while.43 = (s32[]{:T(128)}, f32[6,144,128]{2,1,0:T(8,128)}, s32[8]{0:T(128)}, s32[]{:T(128)}, s32[8]{0:T(128)}, /*index=5*/bf16[8,3,8,16,3072]{4,3,2,1,0:T(8,12...) while((s32[]{:T(128)}, f32[6,144,128]{2,1,0:T(8,128)}, ...), condition=%wide.region_11.12_spmd.clone, body=%wide.region_7.11_spmd.clone.sunk | while | flops 257089568 | bytes 18095392 | solution.py:60
  366.9 11.0 %conditional.10 = (f32[6,144,128]{2,1,0:T(8,128)}) conditional(s32[]{:T(128)} %convert_element_type.77, f32[6,144,128]{2,1,0:T(8,128)} %get-tuple-element.945, (s32[4,12,8,16]{3,2,1,0:T(8,128)S(1)}, s32[]{:T(128)}, s32[8]{0:T(128)}, bf16[8,3,8,16,3072]{4,3,2,1,0:T(8,128)(2,1)}, s32[]{:T(128)}, /*index=5*/bf16[144,6,128]{2,0,1:T(8,128)(2,1)}, ...), branch_computations={%region_8.8_spmd, %region_9.10_spmd} | conditional | flops 257089568 | bytes 18095118 | solution.py:142
  375.2 2.7 fusion.23
  396.7 2.1 collective-permute-start.6
  403.6 2.9 collective-permute-done.7
  407.4 177.5 %all_gather.3 = f32[8,3,8,16,12]{3,2,4,1,0:T(8,128)S(1)} all-gather(f32[1,3,8,16,12]{3,2,4,1,0:T(8,128)S(1)} %copy.93), channel_id=1, replica_groups=mesh['span'=8,'ha'=8,'wa'=4] {'span'}, dimensions={0}, use_global_device_ids=true | all-gather | bytes 165888 | tf_op jit(solution)/shard_map/all_gather | solution.py:195
  586.9 123.1 %while.44 = (s32[]{:T(128)}, f32[144,6,128]{2,0,1:T(8,128)S(1)}, f32[144,6,128]{2,0,1:T(8,128)}, s32[8]{0:T(128)S(1)}, s32[]{:T(128)}, /*index=5*/bf16[8,3,8,16,...) while((s32[]{:T(128)}, f32[144,6,128]{2,0,1:T(8,128)S(1)}, ...), condition=%wide.region_16.17_spmd.clone, body=%wide.region_13.16_spmd.clone.sunk | while | flops 342282240 | bytes 23095652 | solution.py:60
  588.8 13.5 %conditional.11 = ((f32[144,6,128]{2,0,1:T(8,128)S(1)}, f32[144,6,128]{2,0,1:T(8,128)})) conditional(s32[]{:T(128)} %convert_element_type.78, (f32[144,6,128]{2,0,1:T(8,128)S(1)}, f32[144,6,128]{2,0,1:T(8,128)}) %tuple.120, (bf16[8,3,8,16,3072]{4,3,2,1,0:T(8,128)(2,1)}, s32[]{:T(128)}, bf16[144,6,128]{2,0,1:T(8,128)(2,1)}, s32[]{:T(128)}, ...), branch_computations={%region_14.14_spmd, %region_15.15_spmd} | conditional | flops 342282240 | bytes 23095408 | solution.py:177
  588.8 2.0 dynamic-slice_bitcast_fusion.2
  597.5 2.6 fusion.40
  600.0 2.2 fusion.41
  604.2 13.5 %conditional.11 = ((f32[144,6,128]{2,0,1:T(8,128)S(1)}, f32[144,6,128]{2,0,1:T(8,128)})) conditional(s32[]{:T(128)} %convert_element_type.78, (f32[144,6,128]{2,0,1:T(8,128)S(1)}, f32[144,6,128]{2,0,1:T(8,128)}) %tuple.120, (bf16[8,3,8,16,3072]{4,3,2,1,0:T(8,128)(2,1)}, s32[]{:T(128)}, bf16[144,6,128]{2,0,1:T(8,128)(2,1)}, s32[]{:T(128)}, ...), branch_computations={%region_14.14_spmd, %region_15.15_spmd} | conditional | flops 342282240 | bytes 23095408 | solution.py:177
  604.2 2.0 dynamic-slice_bitcast_fusion.2
  612.8 2.6 fusion.40
  615.4 2.2 fusion.41
  619.5 13.5 %conditional.11 = ((f32[144,6,128]{2,0,1:T(8,128)S(1)}, f32[144,6,128]{2,0,1:T(8,128)})) conditional(s32[]{:T(128)} %convert_element_type.78, (f32[144,6,128]{2,0,1:T(8,128)S(1)}, f32[144,6,128]{2,0,1:T(8,128)}) %tuple.120, (bf16[8,3,8,16,3072]{4,3,2,1,0:T(8,128)(2,1)}, s32[]{:T(128)}, bf16[144,6,128]{2,0,1:T(8,128)(2,1)}, s32[]{:T(128)}, ...), branch_computations={%region_14.14_spmd, %region_15.15_spmd} | conditional | flops 342282240 | bytes 23095408 | solution.py:177
  619.6 2.0 dynamic-slice_bitcast_fusion.2
  628.2 2.6 fusion.40
  630.8 2.2 fusion.41
  634.9 13.5 %conditional.11 = ((f32[144,6,128]{2,0,1:T(8,128)S(1)}, f32[144,6,128]{2,0,1:T(8,128)})) conditional(s32[]{:T(128)} %convert_element_type.78, (f32[144,6,128]{2,0,1:T(8,128)S(1)}, f32[144,6,128]{2,0,1:T(8,128)}) %tuple.120, (bf16[8,3,8,16,3072]{4,3,2,1,0:T(8,128)(2,1)}, s32[]{:T(128)}, bf16[144,6,128]{2,0,1:T(8,128)(2,1)}, s32[]{:T(128)}, ...), branch_computations={%region_14.14_spmd, %region_15.15_spmd} | conditional | flops 342282240 | bytes 23095408 | solution.py:177
  635.0 2.0 dynamic-slice_bitcast_fusion.2
  643.6 2.6 fusion.40
  646.2 2.2 fusion.41
  650.3 13.5 %conditional.11 = ((f32[144,6,128]{2,0,1:T(8,128)S(1)}, f32[144,6,128]{2,0,1:T(8,128)})) conditional(s32[]{:T(128)} %convert_element_type.78, (f32[144,6,128]{2,0,1:T(8,128)S(1)}, f32[144,6,128]{2,0,1:T(8,128)}) %tuple.120, (bf16[8,3,8,16,3072]{4,3,2,1,0:T(8,128)(2,1)}, s32[]{:T(128)}, bf16[144,6,128]{2,0,1:T(8,128)(2,1)}, s32[]{:T(128)}, ...), branch_computations={%region_14.14_spmd, %region_15.15_spmd} | conditional | flops 342282240 | bytes 23095408 | solution.py:177
  650.3 2.0 dynamic-slice_bitcast_fusion.2
  659.0 2.6 fusion.40
  661.6 2.2 fusion.41
  665.7 13.5 %conditional.11 = ((f32[144,6,128]{2,0,1:T(8,128)S(1)}, f32[144,6,128]{2,0,1:T(8,128)})) conditional(s32[]{:T(128)} %convert_element_type.78, (f32[144,6,128]{2,0,1:T(8,128)S(1)}, f32[144,6,128]{2,0,1:T(8,128)}) %tuple.120, (bf16[8,3,8,16,3072]{4,3,2,1,0:T(8,128)(2,1)}, s32[]{:T(128)}, bf16[144,6,128]{2,0,1:T(8,128)(2,1)}, s32[]{:T(128)}, ...), branch_computations={%region_14.14_spmd, %region_15.15_spmd} | conditional | flops 342282240 | bytes 23095408 | solution.py:177
  665.7 2.0 dynamic-slice_bitcast_fusion.2
  674.4 2.6 fusion.40
  677.0 2.2 fusion.41
  681.1 13.5 %conditional.11 = ((f32[144,6,128]{2,0,1:T(8,128)S(1)}, f32[144,6,128]{2,0,1:T(8,128)})) conditional(s32[]{:T(128)} %convert_element_type.78, (f32[144,6,128]{2,0,1:T(8,128)S(1)}, f32[144,6,128]{2,0,1:T(8,128)}) %tuple.120, (bf16[8,3,8,16,3072]{4,3,2,1,0:T(8,128)(2,1)}, s32[]{:T(128)}, bf16[144,6,128]{2,0,1:T(8,128)(2,1)}, s32[]{:T(128)}, ...), branch_computations={%region_14.14_spmd, %region_15.15_spmd} | conditional | flops 342282240 | bytes 23095408 | solution.py:177
  681.1 2.0 dynamic-slice_bitcast_fusion.2
  689.8 2.6 fusion.40
  692.4 2.2 fusion.41
  696.5 13.5 %conditional.11 = ((f32[144,6,128]{2,0,1:T(8,128)S(1)}, f32[144,6,128]{2,0,1:T(8,128)})) conditional(s32[]{:T(128)} %convert_element_type.78, (f32[144,6,128]{2,0,1:T(8,128)S(1)}, f32[144,6,128]{2,0,1:T(8,128)}) %tuple.120, (bf16[8,3,8,16,3072]{4,3,2,1,0:T(8,128)(2,1)}, s32[]{:T(128)}, bf16[144,6,128]{2,0,1:T(8,128)(2,1)}, s32[]{:T(128)}, ...), branch_computations={%region_14.14_spmd, %region_15.15_spmd} | conditional | flops 342282240 | bytes 23095408 | solution.py:177
  696.5 2.0 dynamic-slice_bitcast_fusion.2
  705.2 2.6 fusion.40
  707.7 2.2 fusion.41
  (263 shorter events, 124.0 us)
Async XLA Ops:
  173.8 61.3 %copy-start = (bf16[8,1,3,4,12,3072]{5,3,4,2,1,0:T(4,128)(2,1)}, bf16[8,1,3,4,12,3072]{5,3,4,2,1,0:T(4,128)(2,1)S(1)}, u32[]{:S(2)}) copy-start(bf16[8,1,3,4,12,3072]{5,3,4,2,1,0:T(4,128)(2,1)S(1)} %all_to_all.5) | copy-start | bytes 21233668
  180.7 42.8 %collective-permute-start = (bf16[8,3,2,12,3072]{4,0,3,2,1:T(8,128)(2,1)S(1)}, bf16[8,3,2,12,3072]{4,0,3,2,1:T(8,128)(2,1)S(1)}, u32[]{:S(2)}, u32[]{:S(2)}) collective-permute-start(bf16[8,3,2,12,3072]{4,0,3,2,1:T(8,128)(2,1)S(1)} %copy.79), channel_id=1, source_target_pairs={{0,4},{4,8},{8,12},{12,16},{16,20},{20,24},{24,28},{1,5},{5,9},{9,... | collective-permute-start | bytes 10616840 | tf_op jit(solution)/shard_map/ppermute | solution.py:15
  186.4 42.9 %collective-permute-start.1 = (bf16[8,3,2,12,3072]{4,0,3,2,1:T(8,128)(2,1)}, bf16[8,3,2,12,3072]{4,0,3,2,1:T(8,128)(2,1)}, u32[]{:S(2)}, u32[]{:S(2)}) collective-permute-start(bf16[8,3,2,12,3072]{4,0,3,2,1:T(8,128)(2,1)} %copy.80), channel_id=1, source_target_pairs={{4,0},{8,4},{12,8},{16,12},{20,16},{24,20},{28,24},{5,1},{9,5},{13... | collective-permute-start | bytes 10616840 | tf_op jit(solution)/shard_map/ppermute | solution.py:18
  235.0 5.3 copy-start.1
  235.0 11.7 %copy-start.6 = (bf16[1,3,4,12,768]{4,2,3,1,0:T(4,128)(2,1)S(1)}, bf16[1,3,4,12,768]{4,2,3,1,0:T(4,128)(2,1)}, u32[]{:S(2)}) copy-start(bf16[1,3,4,12,768]{4,2,3,1,0:T(4,128)(2,1)} %param.18) | copy-start | bytes 663556
  235.1 12.4 %copy-start.7 = (bf16[1,3,4,12,768]{4,2,3,1,0:T(4,128)(2,1)S(1)}, bf16[1,3,4,12,768]{4,2,3,1,0:T(4,128)(2,1)}, u32[]{:S(2)}) copy-start(bf16[1,3,4,12,768]{4,2,3,1,0:T(4,128)(2,1)} %param.21) | copy-start | bytes 663556
  235.1 13.2 %copy-start.8 = (bf16[1,3,4,12,768]{4,2,3,1,0:T(4,128)(2,1)S(1)}, bf16[1,3,4,12,768]{4,2,3,1,0:T(4,128)(2,1)}, u32[]{:S(2)}) copy-start(bf16[1,3,4,12,768]{4,2,3,1,0:T(4,128)(2,1)} %param.19) | copy-start | bytes 663556
  235.1 13.9 %copy-start.9 = (bf16[1,3,4,12,768]{4,2,3,1,0:T(4,128)(2,1)S(1)}, bf16[1,3,4,12,768]{4,2,3,1,0:T(4,128)(2,1)}, u32[]{:S(2)}) copy-start(bf16[1,3,4,12,768]{4,2,3,1,0:T(4,128)(2,1)} %param.20) | copy-start | bytes 663556
  240.4 54.6 %collective-permute-start.2 = (bf16[8,3,8,2,3072]{4,2,3,1,0:T(8,128)(2,1)}, bf16[8,3,8,2,3072]{4,2,3,1,0:T(8,128)(2,1)}, u32[]{:S(2)}, u32[]{:S(2)}) collective-permute-start(bf16[8,3,8,2,3072]{4,2,3,1,0:T(8,128)(2,1)} %get-tuple-element.644), channel_id=1, source_target_pairs={{0,1},{1,2},{2,3},{4,5},{5,6},{6,7},{8,9},{9,10},{10,11},{12,13},{... | collective-permute-start | bytes 7077896 | tf_op jit(solution)/shard_map/ppermute | solution.py:15
  245.3 55.8 %collective-permute-start.3 = (bf16[8,3,8,2,3072]{4,2,3,1,0:T(8,128)(2,1)}, bf16[8,3,8,2,3072]{4,2,3,1,0:T(8,128)(2,1)}, u32[]{:S(2)}, u32[]{:S(2)}) collective-permute-start(bf16[8,3,8,2,3072]{4,2,3,1,0:T(8,128)(2,1)} %get-tuple-element.645), channel_id=1, source_target_pairs={{1,0},{2,1},{3,2},{5,4},{6,5},{7,6},{9,8},{10,9},{11,10},{13,12},{... | collective-permute-start | bytes 7077896 | tf_op jit(solution)/shard_map/ppermute | solution.py:18
  249.7 21.0 %copy-start.12 = (s32[6]{0:T(128)S(1)}, s32[6]{0:T(128)}, u32[]{:S(2)}) copy-start(s32[6]{0:T(128)} %param.22) | copy-start | bytes 76
  257.4 10.6 %copy-start.13 = (pred[128]{0:T(512)(128)(4,1)S(1)}, pred[128]{0:T(512)(128)(4,1)}, u32[]{:S(2)}) copy-start(pred[128]{0:T(512)(128)(4,1)} %and.135) | copy-start | bytes 388
  315.0 12.7 %copy-start.2 = (s32[4,12,8,16]{3,2,1,0:T(8,128)S(1)}, s32[4,12,8,16]{3,2,1,0:T(8,128)}, u32[]{:S(2)}) copy-start(s32[4,12,8,16]{3,2,1,0:T(8,128)} %broadcast_maximum_fusion) | copy-start | bytes 73732
  357.3 38.4 %collective-permute-start.4 = (f32[1,3,2,12,12]{3,2,1,4,0:T(2,128)}, f32[1,3,2,12,12]{3,2,1,4,0:T(2,128)}, u32[]{:S(2)}, u32[]{:S(2)}) collective-permute-start(f32[1,3,2,12,12]{3,2,1,4,0:T(2,128)} %get-tuple-element.652), channel_id=1, source_target_pairs={{0,4},{4,8},{8,12},{12,16},{16,20},{20,24},{24,28},{1,5},{5,9},{9,... | collective-permute-start | bytes 10376 | tf_op jit(solution)/shard_map/ppermute | solution.py:15
  359.5 36.2 %collective-permute-start.5 = (f32[1,3,2,12,12]{3,2,1,4,0:T(2,128)}, f32[1,3,2,12,12]{3,2,1,4,0:T(2,128)}, u32[]{:S(2)}, u32[]{:S(2)}) collective-permute-start(f32[1,3,2,12,12]{3,2,1,4,0:T(2,128)} %get-tuple-element.653), channel_id=1, source_target_pairs={{4,0},{8,4},{12,8},{16,12},{20,16},{24,20},{28,24},{5,1},{9,5},{13... | collective-permute-start | bytes 10376 | tf_op jit(solution)/shard_map/ppermute | solution.py:18
  368.8 0.9 copy-start.5
  370.1 5.1 copy-start.11
  395.7 6.7 copy-start.10
  396.7 6.8 collective-permute-start.6
  398.9 7.5 %collective-permute-start.7 = (f32[1,3,8,2,12]{3,2,1,4,0:T(8,128)S(1)}, f32[1,3,8,2,12]{3,2,1,4,0:T(8,128)S(1)}, u32[]{:S(2)}, u32[]{:S(2)}) collective-permute-start(f32[1,3,8,2,12]{3,2,1,4,0:T(8,128)S(1)} %get-tuple-element.651), channel_id=1, source_target_pairs={{1,0},{2,1},{3,2},{5,4},{6,5},{7,6},{9,8},{10,9},{11,10},{13,12},{... | collective-permute-start | bytes 6920 | tf_op jit(solution)/shard_map/ppermute | solution.py:18
  588.8 2.0 copy-start.3
  600.0 2.2 copy-start.4
  604.2 2.0 copy-start.3
  615.4 2.2 copy-start.4
  619.6 2.0 copy-start.3
  630.8 2.2 copy-start.4
  634.9 2.0 copy-start.3
  646.2 2.2 copy-start.4
  650.3 2.0 copy-start.3
  661.6 2.2 copy-start.4
  665.7 2.0 copy-start.3
  677.0 2.2 copy-start.4
  681.1 2.0 copy-start.3
  692.4 2.2 copy-start.4
  696.5 2.0 copy-start.3
  707.7 2.2 copy-start.4
